TPU v7x, 32 devices: a whole 2x2x4 slice. The times are simulated.
32 devices in a mesh: groups: 2 (over x), ep: 16 (over z, y, core).
Axes of the slice: x: 2, y: 2, z: 4, core: 2. Of those that a mesh axis runs over, the one named last changes fastest.
Arguments:
- resid: bfloat16 [4096, 2048], P(('groups', 'ep')), parts along dimension 0, may hold values from -12 to 12
- norm_gain: float32 [2048], replicated, may hold values from 0.1 to 1.9
- expert_ids: int32 [4096, 8], P(('groups', 'ep')), parts along dimension 0, may hold values from 0 to 15, as said below
- route_weights: float32 [4096, 8], P(('groups', 'ep')), parts along dimension 0, may hold values from 0.05 to 1
- w_in: bfloat16 [16, 2048, 1536], P('ep'), may hold values from -0.125 to 0.125
- w_out: bfloat16 [16, 768, 2048], P('ep'), may hold values from -0.21875 to 0.21875
Outputs:
- layer_out: bfloat16 [4096, 2048], P(('groups', 'ep')), parts along dimension 0
There are 2 independent parts, one for each index of `groups`. A program takes and returns all parts, laid end to end along the dimension named above; an argument that names none is the same for every part. Nothing has to cross between parts.
Inputs may be any that keep to these rules, and one draw needn't show every extreme that they name: `expert_ids`: each row names 8 different experts. Among the rows of one device no expert is named by more than 96 rows, and in every draw one expert is named by exactly 96 rows of every device.
All inputs are finite; a program needn't handle non-finite values.
Results may differ from a plain program's by a relative error of at most 0.0053.
Values may be sent and summed in bfloat16 or wider, within the bound.
A program may use at most 128 MiB of HBM per device.

v0:
```python
import functools

import jax
import jax.numpy as jnp
from jax import lax
from jax.experimental import pallas as pl
from jax.experimental.pallas import tpu as pltpu
from jax.sharding import PartitionSpec as P


PLANE = 4
PARTS = 2
LAG = 2
MESH = pl.DeviceIdType.MESH


def flip(index, bits):
    bit = 1
    while bit <= bits:
        if bits & bit:
            index = index + bit - 2 * bit * ((index // bit) % 2)
        bit *= 2
    return index


def moe_kernel(
    count, resid_ref, gain_ref, ids_ref, route_ref, win_hbm, wout_hbm, o_ref,
    gathered, table_ref, weights, weight_cols, win, wout, hidden, partial, from_core, from_y,
    from_z, from_near,
    load_sem, table_send, table_recv, z_send, z_recv, y_send, y_recv, core_send, core_recv,
    fwd_send, fwd_recv, rc_send, rc_recv, ry_send, ry_recv, rz_send, rz_recv, rn_send, rn_recv,
):
    rows, width = resid_ref.shape
    units = wout.shape[0]
    planes = count // PLANE
    part = rows // PARTS
    me = lax.axis_index("ep")
    z, q = me // PLANE, me % PLANE
    y, c = q // 2, q % 2
    core_mate = z * PLANE + flip(q, 1)
    y_mate = z * PLANE + flip(q, 2)

    def remote(src, dst, send, recv, target):
        return pltpu.make_async_remote_copy(
            src_ref=src, dst_ref=dst, send_sem=send, recv_sem=recv,
            device_id={"ep": target}, device_id_type=MESH,
        )

    load_in = pltpu.make_async_copy(win_hbm.at[0], win, load_sem.at[0])
    load_out = pltpu.make_async_copy(wout_hbm.at[0], wout, load_sem.at[1])
    load_in.start()
    load_out.start()

    barrier = pltpu.get_barrier_semaphore()
    for k in range(1, count):
        pl.semaphore_signal(
            barrier, inc=1, device_id={"ep": lax.rem(me + k, count)}, device_id_type=MESH
        )

    step = 16

    for h in range(PARTS):

        @pl.loop(0, part // step)
        def _(i, h=h):
            at = pl.ds(pl.multiple_of(i * step, step), step)
            wide = resid_ref[pl.ds(pl.multiple_of(h * part + i * step, step), step), :].astype(
                jnp.float32
            )
            scale = lax.rsqrt(jnp.mean(wide * wide, axis=-1, keepdims=True) + 1e-06)
            gathered[z * PARTS + h, q, at, :] = (wide * scale * gain_ref[...]).astype(jnp.bfloat16)

    mix = route_ref[...] / jnp.sum(route_ref[...], axis=0, keepdims=True)
    for e in range(count):
        table_ref[e] = jnp.sum(jnp.where(ids_ref[...] == e, mix, 0.0), axis=0, keepdims=True)
    weights[me] = jnp.sum(jnp.where(ids_ref[...] == me, mix, 0.0), axis=0, keepdims=True)
    pl.semaphore_wait(barrier, count - 1)

    started = []

    def begin(copy):
        copy.start()
        started.append(copy)
        return copy

    low, high = z, planes - 1 - z
    near = jnp.minimum(low, high)
    side = jnp.where(low < high, -1, 1)

    def visit(k):
        if k == 0:
            return z
        paired = (side if k % 2 else -side) * ((k + 1) // 2)
        return z + jnp.where(k <= 2 * near, paired, -side * (k - near))

    plane_of = [visit(k) for k in range(planes)]
    near_planes = [False, True, near >= 1] + [False] * planes
    units_all = planes * PARTS
    is_near = [near_planes[s // PARTS] for s in range(units_all)]
    piece_of = [plane_of[s // PARTS] * PARTS + s % PARTS for s in range(units_all)]

    def when(condition, run):
        if condition is True:
            run()
        elif condition is not False:
            pl.when(condition)(run)

    def negate(condition):
        return not condition if isinstance(condition, bool) else jnp.logical_not(condition)

    to_y, to_core, to_fwd = {}, {}, {}
    red_core, red_y, red_z = {}, {}, {}
    guarded = []

    def begin_if(condition, copy):
        @pl.when(condition)
        def _():
            copy.start()

        guarded.append((condition, copy))

    def spread(s):
        src = dst = gathered.at[piece_of[s], q]
        to_y[s] = begin(remote(src, dst, y_send.at[s], y_recv.at[s], y_mate))
        to_core[s] = begin(remote(src, dst, core_send.at[s], core_recv.at[s], core_mate))

    def forward(s):
        to_y[s].wait_recv()
        block = gathered.at[piece_of[s], flip(q, 2)]
        to_fwd[s] = begin(remote(block, block, fwd_send.at[s], fwd_recv.at[s], core_mate))

    def z_copy(p, src, send, target_plane):
        return remote(
            src, gathered.at[p, q], z_send.at[send], z_recv.at[p], target_plane * PLANE + q
        )

    for s in range(PARTS):
        p = piece_of[s]
        spread(s)
        begin_if(z > 0, z_copy(p, gathered.at[p, q], s, jnp.maximum(z - 1, 0)))
        begin_if(
            z < planes - 1,
            z_copy(p, gathered.at[p, q], units_all + s, jnp.minimum(z + 1, planes - 1)),
        )
    tables = []
    for k in range(1, count):
        target = lax.rem(me + k, count)
        tables.append(
            begin(
                remote(
                    table_ref.at[target], weights.at[me],
                    table_send.at[k - 1], table_recv.at[k - 1], target,
                )
            )
        )
    for slot, there in ((0, z > 0), (1, z < planes - 1)):

        @pl.when(jnp.logical_not(there))
        def _(slot=slot):
            for h in range(PARTS):
                from_near[slot * PARTS + h] = jnp.zeros(from_near.shape[1:], jnp.bfloat16)

    if planes > 2:

        @pl.when(near_planes[2])
        def _():
            for h in range(PARTS):
                from_z[plane_of[2] * PARTS + h] = jnp.zeros(from_z.shape[1:], jnp.bfloat16)

    def arrive(s):
        if s >= units_all:
            return
        p, plane = piece_of[s], plane_of[s // PARTS]
        block = gathered.at[p, q]
        z_copy(p, block, s, plane).wait_recv()
        onward = jnp.where(plane < z, z + 1, z - 1)
        inside = jnp.logical_and(onward >= 0, onward < planes)
        begin_if(inside, z_copy(p, block, s, jnp.clip(onward, 0, planes - 1)))
        spread(s)

    tile_in = 256 if units % 256 == 0 else units
    tile_out = 512 if width % 512 == 0 else width

    def experts(s):
        plane, h = plane_of[s // PARTS], s % PARTS
        eye = lax.broadcasted_iota(jnp.int32, (rows, rows), 0) == lax.broadcasted_iota(
            jnp.int32, (rows, rows), 1
        )
        for k in range(PLANE):
            lane = jnp.broadcast_to(weights[plane * PLANE + k], (rows, rows))
            column = jnp.sum(jnp.where(eye, lane, 0.0), axis=1, keepdims=True)
            weight_cols[pl.ds(k * part, part), :] = jnp.broadcast_to(
                column[h * part : (h + 1) * part], (part, 128)
            )

        @pl.loop(0, units // tile_in)
        def _(j):
            gate_at = pl.multiple_of(j * tile_in, 128)
            up_at = pl.multiple_of(units + j * tile_in, 128)
            block = gathered[piece_of[s]].reshape(PLANE * part, width)
            gate = jnp.dot(
                block, win[:, pl.ds(gate_at, tile_in)], preferred_element_type=jnp.float32
            )
            up = jnp.dot(block, win[:, pl.ds(up_at, tile_in)], preferred_element_type=jnp.float32)
            act = gate / (1.0 + jnp.exp(-gate)) * up
            hidden[:, pl.ds(gate_at, tile_in)] = act.astype(jnp.bfloat16)

        @pl.loop(0, width // tile_out)
        def _(j):
            at = pl.multiple_of(j * tile_out, 128)
            made = jnp.dot(
                hidden[...], wout[:, pl.ds(at, tile_out)], preferred_element_type=jnp.float32
            )
            made = made.astype(jnp.bfloat16).astype(jnp.float32)
            for k in range(PLANE):
                cols = weight_cols[pl.ds(k * part, part), :]
                pieces = [
                    made[k * part : (k + 1) * part, i * 128 : (i + 1) * 128] * cols
                    for i in range(tile_out // 128)
                ]
                partial[s, k % 2, k // 2, :, pl.ds(at, tile_out)] = jnp.concatenate(
                    pieces, axis=1
                ).astype(jnp.bfloat16)

    def reduce_core(s):
        red_core[s] = begin(
            remote(
                partial.at[s, flip(c, 1)], from_core.at[s], rc_send.at[s], rc_recv.at[s], core_mate
            )
        )

    def y_copy(s):
        return remote(
            partial.at[s, c, flip(y, 1)], from_y.at[s], ry_send.at[s], ry_recv.at[s], y_mate
        )

    def far_copy(s, source):
        return remote(
            partial.at[s, c, y], from_z.at[source], rz_send.at[s], rz_recv.at[source],
            plane_of[s // PARTS] * PLANE + q,
        )

    def near_copy(s, slot):
        return remote(
            partial.at[s, c], from_near.at[slot], rn_send.at[s], rn_recv.at[slot],
            plane_of[s // PARTS] * PLANE + q,
        )

    def reduce_y(s):
        red_core[s].wait_recv()
        if s < PARTS:
            for slot, there in ((0, z > 0), (1, z < planes - 1)):

                @pl.when(there)
                def _(slot=slot):
                    near_copy(s, slot * PARTS + s).wait_recv()

        @pl.loop(0, part // step)
        def _(i):
            at = pl.ds(pl.multiple_of(i * step, step), step)
            for k in range(2):
                total = partial[s, c, k, at, :].astype(jnp.float32) + from_core[
                    s, k, at, :
                ].astype(jnp.float32)
                if s < PARTS:
                    for slot in range(2):
                        total = total + from_near[slot * PARTS + s, k, at, :].astype(jnp.float32)
                partial[s, c, k, at, :] = total.astype(jnp.bfloat16)

        side_slot = jnp.where(plane_of[s // PARTS] > z, 0, PARTS)
        when(is_near[s], lambda: near_copy(s, side_slot + s % PARTS).start())
        when(negate(is_near[s]), lambda: y_copy(s).start())

    def reduce_z(s):
        def run():
            y_copy(s).wait_recv()

            @pl.loop(0, part // step)
            def _(i):
                at = pl.ds(pl.multiple_of(i * step, step), step)
                total = partial[s, c, y, at, :].astype(jnp.float32) + from_y[s, at, :].astype(
                    jnp.float32
                )
                partial[s, c, y, at, :] = total.astype(jnp.bfloat16)

            far_copy(s, z * PARTS + s % PARTS).start()

        when(negate(is_near[s]), run)

    arrive(PARTS)
    forward(0)
    load_in.wait()
    load_out.wait()
    for copy in tables:
        copy.wait_recv()
    arrive(PARTS + 1)
    for s in range(units_all):
        to_core[s].wait_recv()
        to_fwd[s].wait_recv()
        experts(s)
        reduce_core(s)
        arrive(s + PARTS + 2)
        if s + 1 < units_all:
            forward(s + 1)
        if s >= PARTS:
            reduce_y(s)
        if s >= 2 * PARTS + LAG:
            reduce_z(s - LAG)
    for s in range(max(units_all - LAG, 2 * PARTS), units_all):
        reduce_z(s)
    for s in range(PARTS):
        reduce_y(s)
    for s in range(PARTS):
        y_copy(s).wait_recv()
    for s in range(2 * PARTS, units_all):
        when(negate(is_near[s]), lambda s=s: far_copy(s, piece_of[s]).wait_recv())

    for h in range(PARTS):

        @pl.loop(0, part // step)
        def _(i, h=h):
            at = pl.ds(pl.multiple_of(i * step, step), step)
            out_at = pl.ds(pl.multiple_of(h * part + i * step, step), step)
            total = partial[h, c, y, at, :].astype(jnp.float32)
            total = total + from_y[h, at, :].astype(jnp.float32)
            for s in range(2, planes):
                total = total + from_z[plane_of[s] * PARTS + h, at, :].astype(jnp.float32)
            o_ref[out_at, :] = (resid_ref[out_at, :].astype(jnp.float32) + total).astype(
                jnp.bfloat16
            )

    for copy in started:
        copy.wait_send()
    for condition, copy in guarded:

        @pl.when(condition)
        def _(copy=copy):
            copy.wait_send()

    for s in range(PARTS):
        y_copy(s).wait_send()
    for s in range(PARTS, units_all):
        when(is_near[s], lambda s=s: near_copy(s, 0).wait_send())

        def sent(s=s):
            y_copy(s).wait_send()
            far_copy(s, z * PARTS + s % PARTS).wait_send()

        when(negate(is_near[s]), sent)


def vmem_bytes(count, rows, width, units):
    block = 2 * rows * width
    return (
        block * (4 * 2 * (count // PLANE) + 8) + 2 * 3 * units * width
        + 2 * PLANE * rows * units + 8 * count * rows * 4
    )


def local(resid, norm_gain, expert_ids, route_weights, w_in, w_out):
    rows, width = resid.shape
    units = w_out.shape[1]
    count = lax.axis_size("ep")
    planes = count // PLANE
    fits = vmem_bytes(count, rows, width, units) <= 44 * 2**20
    if count % PLANE or planes < 2 or planes & (planes - 1) or rows != 128 or not fits:
        return local_wide(resid, norm_gain, expert_ids, route_weights, w_in, w_out)
    part, pieces = rows // PARTS, planes * PARTS
    vmem = pl.BlockSpec(memory_space=pltpu.VMEM)
    hbm = pl.BlockSpec(memory_space=pl.ANY)
    bf16 = jnp.bfloat16
    dma = pltpu.SemaphoreType.DMA
    return pl.pallas_call(
        functools.partial(moe_kernel, count),
        out_shape=jax.ShapeDtypeStruct((rows, width), bf16),
        in_specs=[vmem, vmem, vmem, vmem, hbm, hbm],
        out_specs=vmem,
        scratch_shapes=[
            pltpu.VMEM((pieces, PLANE, part, width), bf16),
            pltpu.VMEM((count, 1, rows), jnp.float32),
            pltpu.VMEM((count, 1, rows), jnp.float32),
            pltpu.VMEM((PLANE * part, 128), jnp.float32),
            pltpu.VMEM((width, 2 * units), bf16),
            pltpu.VMEM((units, width), bf16),
            pltpu.VMEM((PLANE * part, units), bf16),
            pltpu.VMEM((pieces, 2, 2, part, width), bf16),
            pltpu.VMEM((pieces, 2, part, width), bf16),
            pltpu.VMEM((pieces, part, width), bf16),
            pltpu.VMEM((pieces, part, width), bf16),
            pltpu.VMEM((2 * PARTS, 2, part, width), bf16),
            dma((2,)),
            dma((count - 1,)),
            dma((count - 1,)),
        ]
        + [dma((pieces + PARTS,))] * 16,
        compiler_params=pltpu.CompilerParams(
            collective_id=0, has_side_effects=True, vmem_limit_bytes=60 * 2**20
        ),
    )(resid, norm_gain[None], expert_ids.T, route_weights.T, w_in, w_out)


def local_wide(resid, norm_gain, expert_ids, route_weights, w_in, w_out):
    token_rows, model_width = resid.shape
    top_count = expert_ids.shape[1]
    ep_devices = lax.axis_size("ep")
    capacity = 3 * token_rows * top_count // (2 * ep_devices)
    weight_in = w_in[0]
    weight_out = w_out[0]
    hidden_units = weight_out.shape[0]
    resid_wide = resid.astype(jnp.float32)
    scale = lax.rsqrt(jnp.mean(resid_wide * resid_wide, axis=-1, keepdims=True) + 1e-06)
    normed = (resid_wide * scale * norm_gain).astype(jnp.bfloat16)
    mix_weights = route_weights / jnp.sum(route_weights, axis=-1, keepdims=True)
    flat_ids = expert_ids.reshape(-1)
    onehot = (flat_ids[:, None] == jnp.arange(ep_devices, dtype=jnp.int32)[None, :]).astype(
        jnp.int32
    )
    position = jnp.sum((jnp.cumsum(onehot, axis=0) - onehot) * onehot, axis=1)
    slot_index = flat_ids * capacity + position
    all_normed, all_ids = (
        lax.all_gather(normed, "ep", axis=0, tiled=True),
        lax.all_gather(expert_ids, "ep", axis=0, tiled=True),
    )
    own_expert = lax.axis_index("ep")
    row_hits = (
        jnp.any(all_ids == own_expert, axis=1).astype(jnp.int32).reshape(ep_devices, token_rows)
    )
    placing = jnp.cumsum(row_hits, axis=1) - row_hits
    target = jnp.where(
        row_hits == 1,
        jnp.arange(ep_devices, dtype=jnp.int32)[:, None] * capacity + placing,
        ep_devices * capacity,
    ).reshape(-1)
    received = (
        jnp.zeros((ep_devices * capacity, model_width), jnp.bfloat16)
        .at[target]
        .set(all_normed, mode="drop")
    )
    block_rows = received.reshape(ep_devices, capacity, model_width)
    rows_flat = block_rows.reshape(-1, model_width)
    projected = jnp.dot(rows_flat, weight_in, preferred_element_type=jnp.float32)
    activated = (jax.nn.silu(projected[:, :hidden_units]) * projected[:, hidden_units:]).astype(
        jnp.bfloat16
    )
    produced = jnp.dot(activated, weight_out, preferred_element_type=jnp.float32).astype(
        jnp.bfloat16
    )
    outputs = produced.reshape(block_rows.shape)
    returned = lax.all_to_all(outputs, "ep", split_axis=0, concat_axis=0, tiled=True).reshape(
        -1, model_width
    )
    picked = returned[slot_index].reshape(token_rows, top_count, model_width).astype(jnp.float32)
    mixed = jnp.sum(mix_weights[:, :, None] * picked, axis=1)
    return (resid_wide + mixed).astype(jnp.bfloat16)


def solution(mesh):
    in_specs = (
        P(("groups", "ep"), None),
        P(),
        P(("groups", "ep"), None),
        P(("groups", "ep"), None),
        P("ep", None, None),
        P("ep", None, None),
    )
    out_specs = P(("groups", "ep"), None)
    return jax.shard_map(local, mesh=mesh, in_specs=in_specs, out_specs=out_specs, check_vma=False)
```

profile of v0, /device:TPU:0, one launch (start us, length us, event | category | flops | bytes accessed | tf_op | source)
XLA Modules:
  0.0 115.2 jit_solution(8213789723659941498)
XLA Ops:
  0.0 113.3 %shard_map.64 = bf16[128,2048]{1,0:T(8,128)(2,1)} custom-call(bf16[128,2048]{1,0:T(8,128)(2,1)} %resid_ref.1, f32[1,2048]{1,0:T(1,128)} %bitcast.3, s32[8,128]{1,0:T(8,128)} %bitcast.4, f32[8,128]{1,0:T(8,128)} %bitcast.5, bf16[1,2048,1536]{2,1,0:T(8,128)(2,1)} %win_hbm.1, bf16[1,768,2048]{2,1,0:T(8,128)(2,1)} %wout_hbm.1), custom_call_target="tpu_custom_call" | custom-call | tf_op jit(solution)/shard_map/pallas_call | solution.py:373
  113.3 1.9 %copy.8 = bf16[128,2048]{1,0:T(8,128)(2,1)} copy(bf16[128,2048]{1,0:T(8,128)(2,1)} %shard_map.64) | data formatting | bytes 1048576
where the time goes:
time: 115 us
  Pallas kernels  113 us (98%)
  local copies, waits for them, and re-layouts  1.88 us (2%)
    pallas_call x1, Pallas kernels, local(): pl.pallas_call(functools.partial(moe_kernel, count), out_shape=jax.ShapeD...  113 us

commit v1 on v0

v1 whole, which is shorter than its diff:
```python
import functools
import math

import jax
import jax.numpy as jnp
from jax import lax
from jax.experimental import pallas as pl
from jax.experimental.pallas import tpu as pltpu
from jax.sharding import PartitionSpec as P


PLANE = 4
PARTS = 2
MESH = pl.DeviceIdType.MESH
PAIRS = ("pA", "pB", "t2p")
SINGLES = ("m1", "mB", "t2", "t3", "far")

END_STEPS = (
    ("zs", 0, "01", (1, 2)), ("yc", 1), ("yc", 2), ("hand", 1), ("zs", 1, "01", (1, 3)),
    ("xa", 1), ("hand", 2), ("yc", 4), ("zz", 1, "01", (1, 3)), ("yc", 0), ("xb", 1), ("xa", 2),
    ("xb", 2), ("hand", 4), ("pair", 2, 1, "01", (1, "pA", 0)), ("xa", 4), ("yc", 6), ("hand", 0),
    ("xb", 4), ("pair", 4, 0, "01", (1, "t2p", 0)), ("yc", 7), ("yc", 5),
    ("pair", 4, 1, "01", (1, "t2p", 0)), ("hand", 6), ("xa", 6), ("xb", 6), ("hand", 7),
    ("sy", 6), ("xa", 7), ("xb", 7), ("hand", 5), ("pf", 3), ("pair", 2, 0, "01", (1, "pA", 0)),
    ("sy", 7), ("xa", 5), ("xb", 5), ("ss", 6, "01", (1, "t3", 0), None), ("c", 3), ("sy", 5),
    ("xa", 3), ("ss", 7, "01", (1, "t3", 1), None), ("xb", 3), ("sy", 3), ("sy", 1, ("pA", 1, 0)),
    ("ss", 5, "01", (1, "t2", 1), None), ("xa", 0), ("xb", 0),
    ("ss", 3, "01", (1, "m1", 1), None), ("sy", 0), ("fin", 1, ("far", 1), ("pA", 1, 1)),
    ("fin", 0, ("far", 0), ("m1", 0)),
)

INNER_STEPS = (
    ("zs", 0, "12", (1, 4)), ("zs", 0, "10", (0, 2)), ("yc", 1), ("zs", 1, "12", (1, 5)),
    ("on", 2, "12", (1, 6)), ("yc", 0), ("hand", 1), ("on", 4, "10", (0, 4)), ("yc", 2),
    ("on", 5, "10", (0, 5)), ("xa", 1), ("c", 4), ("c", 5), ("on", 3, "12", (1, 7)), ("hand", 0),
    ("xb", 1), ("yc", 6), ("on", 6, "10", (0, 6)), ("hand", 2), ("pf", 3), ("c", 3), ("xa", 2),
    ("on", 7, "10", (0, 7)), ("xb", 2), ("hand", 6), ("zz", 0, "12", (1, 4)),
    ("zz", 1, "10", (0, 3)), ("sy", 2), ("yc", 7), ("xa", 3), ("xb", 3), ("sy", 1),
    ("zs", 1, "10", (0, 3)), ("zz", 1, "12", (1, 5)), ("xa", 6), ("pf", 4), ("xb", 6), ("xa", 4),
    ("hand", 7), ("pair", 3, 0, "10", (0, "pA", 1)), ("sy", 6), ("xb", 4),
    ("ss", 2, "10", (0, "m1", 0), None), ("pair", 4, 1, "12", (1, "pB", 0), ("t2p", 0, 1)),
    ("xa", 7), ("pf", 5), ("pair", 3, 1, "10", (0, "pA", 1)), ("xb", 7), ("sy", 7),
    ("pair", 4, 0, "12", (1, "pB", 0), ("t2p", 0, 0)), ("xa", 5), ("xb", 5),
    ("ss", 6, "110", (0, "far", 0), ("t3", 0)), ("sy", 5, None), ("xa", 0), ("xb", 0),
    ("ss", 7, "110", (0, "far", 1), ("t3", 1)), ("sy", 0, ("pA", 0, 0), ("pB", 0, 0)),
    ("ss", 5, "12", (1, "mB", 1), ("t2", 1)), ("fin", 0, ("pA", 0, 1), ("pB", 0, 1)),
    ("fin", 1, ("m1", 1), ("mB", 1)),
)


def flip(index, bits):
    bit = 1
    while bit <= bits:
        if bits & bit:
            index = index + bit - 2 * bit * ((index // bit) % 2)
        bit *= 2
    return index


def moe_kernel(
    count, resid_ref, gain_ref, ids_ref, route_ref, win_hbm, wout_hbm, o_hbm,
    gathered, table_ref, weights, weight_cols, win, wout, hidden, partial, from_core, from_y,
    pair_in, single_in, out_buf,
    load_sem, out_sem, table_send, table_recv, z_send, z_recv, zz_send, zz_recv, y_send, y_recv,
    core_send, core_recv, fwd_send, fwd_recv, rc_send, rc_recv, ry_send, ry_recv,
    pair_send, pair_recv, single_send, single_recv,
):
    rows, width = resid_ref.shape
    units = wout.shape[0]
    planes = count // PLANE
    part = rows // PARTS
    tiles = rc_send.shape[1]
    me = lax.axis_index("ep")
    z, q = me // PLANE, me % PLANE
    y, c = q // 2, q % 2
    end = jnp.logical_or(z == 0, z == planes - 1)
    other_q, other_y, core_q = flip(q, 2), flip(y, 1), flip(q, 1)
    cols = (other_y, y)
    pieces = planes * PARTS
    step = 16

    def remote(src, dst, send, recv, plane, spot):
        return pltpu.make_async_remote_copy(
            src_ref=src, dst_ref=dst, send_sem=send, recv_sem=recv,
            device_id={"ep": plane * PLANE + spot}, device_id_type=MESH,
        )

    load_in = pltpu.make_async_copy(win_hbm.at[0], win, load_sem.at[0])
    load_out = pltpu.make_async_copy(wout_hbm.at[0], wout, load_sem.at[1])
    load_in.start()
    load_out.start()

    barrier = pltpu.get_barrier_semaphore()
    for k in range(1, count):
        pl.semaphore_signal(
            barrier, inc=1, device_id={"ep": lax.rem(me + k, count)}, device_id_type=MESH
        )

    for h in range(PARTS):

        @pl.loop(0, part // step)
        def _(i, h=h):
            at = pl.ds(pl.multiple_of(i * step, step), step)
            wide = resid_ref[pl.ds(pl.multiple_of(h * part + i * step, step), step), :].astype(
                jnp.float32
            )
            scale = lax.rsqrt(jnp.mean(wide * wide, axis=-1, keepdims=True) + 1e-06)
            gathered[z * PARTS + h, q, at, :] = (wide * scale * gain_ref[...]).astype(jnp.bfloat16)

    mix = route_ref[...] / jnp.sum(route_ref[...], axis=0, keepdims=True)
    for e in range(count):
        table_ref[e] = jnp.sum(jnp.where(ids_ref[...] == e, mix, 0.0), axis=0, keepdims=True)
    weights[me] = jnp.sum(jnp.where(ids_ref[...] == me, mix, 0.0), axis=0, keepdims=True)
    pl.semaphore_wait(barrier, count - 1)

    def table_copy(k):
        target = lax.rem(me + k, count)
        return pltpu.make_async_remote_copy(
            src_ref=table_ref.at[target], dst_ref=weights.at[me],
            send_sem=table_send.at[k - 1], recv_sem=table_recv.at[k - 1],
            device_id={"ep": target}, device_id_type=MESH,
        )

    for k in range(1, count):
        table_copy(k).start()

    def columns_of_weights():
        for k in range(1, count):
            table_copy(k).wait_recv()

        @pl.loop(0, count)
        def _(i):
            lane = jnp.broadcast_to(weights[i], (rows, rows))
            eye = lax.broadcasted_iota(jnp.int32, (rows, rows), 0) == lax.broadcasted_iota(
                jnp.int32, (rows, rows), 1
            )
            column = jnp.sum(jnp.where(eye, lane, 0.0), axis=1, keepdims=True)
            for h in range(PARTS):
                weight_cols[(i // PLANE) * PARTS + h, i % PLANE] = jnp.broadcast_to(
                    column[h * part : (h + 1) * part], (part, 128)
                )

    tile_in = 256 if units % 256 == 0 else units
    tile_out = width // tiles

    def play(at_end, steps):
        mate, across, beyond = flip(z, 1), flip(z, 3), flip(z, 2)
        plane_of = [z, mate, beyond, across] if at_end else [z, mate, across, beyond]
        piece_of = [plane_of[s // PARTS] * PARTS + s % PARTS for s in range(pieces)]
        to_plane = {"01": mate, "10": mate, "12": across, "012": beyond, "110": beyond}
        started, waited = [], set()

        def begin(copy):
            copy.start()
            started.append(copy)

        def own_column(s):
            return gathered.at[piece_of[s], q]

        def other_column(s):
            return gathered.at[piece_of[s], other_q]

        def tile_copy(s, j):
            at = pl.ds(pl.multiple_of(j * tile_out, 128), tile_out)
            return remote(
                partial.at[s, flip(c, 1), :, :, at], from_core.at[s, :, :, at],
                rc_send.at[s, j], rc_recv.at[s, j], z, core_q,
            )

        def arrived(name, *spot):
            if name in PAIRS:
                return pair_in.at[PAIRS.index(name), spot[0], spot[1]]
            return single_in.at[SINGLES.index(name), spot[0]]

        def wait(name, *spot):
            if (name,) + spot in waited:
                return
            waited.add((name,) + spot)
            s = spot[0]
            if name == "z":
                ref, send, recv = own_column(s), z_send.at[0], z_recv.at[piece_of[s]]
            elif name == "zz":
                ref, send, recv = other_column(s), zz_send.at[0], zz_recv.at[s]
            elif name == "y":
                ref, send, recv = own_column(s), y_send.at[s], y_recv.at[s]
            elif name == "c":
                ref, send, recv = own_column(s), core_send.at[s], core_recv.at[s]
            elif name == "f":
                ref, send, recv = other_column(s), fwd_send.at[s], fwd_recv.at[s]
            elif name == "ry":
                ref, send, recv = from_y.at[s], ry_send.at[s], ry_recv.at[s]
            elif name in PAIRS:
                kind = PAIRS.index(name)
                ref = arrived(name, *spot)
                send, recv = pair_send.at[0], pair_recv.at[kind, spot[0], spot[1]]
            elif name in SINGLES:
                kind = SINGLES.index(name)
                ref = arrived(name, *spot)
                send, recv = single_send.at[0], single_recv.at[kind, spot[0]]
            else:
                for j in range(tiles):
                    tile_copy(s, j).wait_recv()
                return
            remote(ref, ref, send, recv, z, core_q).wait_recv()

        def core(s):
            begin(
                remote(
                    own_column(s), own_column(s), core_send.at[s], core_recv.at[s], z, core_q
                )
            )

        def hand(s):
            begin(
                remote(
                    other_column(s), other_column(s), fwd_send.at[s], fwd_recv.at[s], z, core_q
                )
            )

        def add_rows(store, loads):
            @pl.loop(0, part // step)
            def _(i):
                at = pl.ds(pl.multiple_of(i * step, step), step)
                total = loads[0][at, :].astype(jnp.float32)
                for ref in loads[1:]:
                    total = total + ref[at, :].astype(jnp.float32)
                store[at, :] = total.astype(jnp.bfloat16)

        def sums(s, side, extras):
            wait("rc", s)
            spot = partial.at[s, c, cols[side]]
            loads = [spot, from_core.at[s, cols[side]]]
            for extra in extras:
                wait(*extra)
                loads.append(from_y.at[s] if extra[0] == "ry" else arrived(*extra))
            add_rows(spot, loads)
            return spot

        def first_matmul(s):
            @pl.loop(0, units // tile_in)
            def _(j):
                gate_at = pl.multiple_of(j * tile_in, 128)
                up_at = pl.multiple_of(units + j * tile_in, 128)
                block = gathered[piece_of[s]].reshape(PLANE * part, width)
                gate = jnp.dot(
                    block, win[:, pl.ds(gate_at, tile_in)], preferred_element_type=jnp.float32
                )
                up = jnp.dot(
                    block, win[:, pl.ds(up_at, tile_in)], preferred_element_type=jnp.float32
                )
                act = gate / (1.0 + jnp.exp(-gate)) * up
                hidden[:, pl.ds(gate_at, tile_in)] = act.astype(jnp.bfloat16)

        def second_matmul(s):
            @pl.loop(0, tiles)
            def _(j):
                at = pl.multiple_of(j * tile_out, 128)
                made = jnp.dot(
                    hidden[...], wout[:, pl.ds(at, tile_out)], preferred_element_type=jnp.float32
                )
                made = made.astype(jnp.bfloat16).astype(jnp.float32)
                for k in range(PLANE):
                    scale = weight_cols[piece_of[s], k]
                    scaled = [
                        made[k * part : (k + 1) * part, i * 128 : (i + 1) * 128] * scale
                        for i in range(tile_out // 128)
                    ]
                    partial[s, k % 2, k // 2, :, pl.ds(at, tile_out)] = jnp.concatenate(
                        scaled, axis=1
                    ).astype(jnp.bfloat16)
                tile_copy(s, j).start()

        def finish(h, extras):
            wait("rc", h)
            wait("ry", h)
            refs = [from_core.at[h, y], from_y.at[h]]
            for extra in extras:
                wait(*extra)
                refs.append(arrived(*extra))

            @pl.loop(0, part // step)
            def _(i):
                at = pl.ds(pl.multiple_of(i * step, step), step)
                out_at = pl.ds(pl.multiple_of(h * part + i * step, step), step)
                total = partial[h, c, y, at, :].astype(jnp.float32)
                for ref in refs:
                    total = total + ref[at, :].astype(jnp.float32)
                out_buf[out_at, :] = (resid_ref[out_at, :].astype(jnp.float32) + total).astype(
                    jnp.bfloat16
                )

            out_at = pl.ds(h * part, part)
            pltpu.make_async_copy(
                out_buf.at[out_at, :], o_hbm.at[out_at, :], out_sem.at[h]
            ).start()

        z_count = zz_count = pair_count = single_count = 0
        loaded = False
        for item in steps:
            kind, s = item[0], item[1]
            if kind in ("zs", "on"):
                if kind == "on":
                    wait("z", s)
                begin(
                    remote(
                        own_column(s), own_column(s), z_send.at[z_count],
                        z_recv.at[piece_of[s]], to_plane[item[2]], q,
                    )
                )
                z_count += 1
            elif kind in ("yc", "c"):
                if s >= PARTS:
                    wait("z", s)
                if kind == "yc":
                    begin(
                        remote(
                            own_column(s), own_column(s), y_send.at[s], y_recv.at[s], z, other_q
                        )
                    )
                core(s)
            elif kind == "hand":
                wait("y", s)
                hand(s)
            elif kind == "pf":
                wait("zz", s)
                hand(s)
            elif kind == "zz":
                wait("y", s)
                begin(
                    remote(
                        other_column(s), other_column(s), zz_send.at[zz_count],
                        zz_recv.at[item[3][1]], to_plane[item[2]], q,
                    )
                )
                zz_count += 1
            elif kind == "xa":
                wait("c", s)
                wait("f", s)
                if not loaded:
                    columns_of_weights()
                    load_in.wait()
                    load_out.wait()
                    loaded = True
                first_matmul(s)
            elif kind == "xb":
                second_matmul(s)
            elif kind == "sy":
                spot = sums(s, 0, [extra for extra in item[2:] if extra])
                begin(remote(spot, from_y.at[s], ry_send.at[s], ry_recv.at[s], z, other_q))
            elif kind == "ss":
                spot = sums(s, 1, [("ry", s)] + [extra for extra in item[4:] if extra])
                where = (SINGLES.index(item[3][1]), item[3][2])
                begin(
                    remote(
                        spot, single_in.at[where[0], where[1]], single_send.at[single_count],
                        single_recv.at[where[0], where[1]], to_plane[item[2]], q,
                    )
                )
                single_count += 1
            elif kind == "pair":
                side = item[2]
                spot = sums(s, side, [extra for extra in item[5:] if extra])
                where = (PAIRS.index(item[4][1]), item[4][2], side)
                begin(
                    remote(
                        spot, pair_in.at[where], pair_send.at[pair_count],
                        pair_recv.at[where], to_plane[item[3]], q,
                    )
                )
                pair_count += 1
            else:
                finish(s, item[2:])
        for copy in started:
            copy.wait_send()
        for s in range(pieces):
            for j in range(tiles):
                tile_copy(s, j).wait_send()

    @pl.when(end)
    def _():
        play(True, END_STEPS)

    @pl.when(jnp.logical_not(end))
    def _():
        play(False, INNER_STEPS)

    for k in range(1, count):
        table_copy(k).wait_send()
    for h in range(PARTS):
        at = pl.ds(h * part, part)
        pltpu.make_async_copy(out_buf.at[at, :], o_hbm.at[at, :], out_sem.at[h]).wait()


def local(resid, norm_gain, expert_ids, route_weights, w_in, w_out):
    rows, width = resid.shape
    units = w_out.shape[1]
    count = lax.axis_size("ep")
    planes = count // PLANE
    part, pieces, tiles = rows // PARTS, planes * PARTS, 4
    bf16 = jnp.bfloat16
    blocks = [
        (pieces, PLANE, part, width), (pieces, 2, 2, part, width), (pieces, 2, part, width),
        (pieces, part, width), (len(PAIRS), PARTS, 2, part, width),
        (len(SINGLES), PARTS, part, width), (rows, width), (width, 2 * units), (units, width),
        (PLANE * part, units),
    ]
    vmem_bytes = sum(2 * math.prod(shape) for shape in blocks) + 4 * 128 * PLANE * part * pieces
    if planes != 4 or count != 16 or rows != 128 or width % 512 or vmem_bytes > 50 * 2**20:
        return local_wide(resid, norm_gain, expert_ids, route_weights, w_in, w_out)
    vmem = pl.BlockSpec(memory_space=pltpu.VMEM)
    hbm = pl.BlockSpec(memory_space=pl.ANY)
    dma = pltpu.SemaphoreType.DMA
    (gathered, partial, from_core, from_y, pair_in, single_in, out_buf, win, wout, hidden) = [
        pltpu.VMEM(shape, bf16) for shape in blocks
    ]
    table = pltpu.VMEM((count, 1, rows), jnp.float32)
    columns = pltpu.VMEM((pieces, PLANE, part, 128), jnp.float32)
    return pl.pallas_call(
        functools.partial(moe_kernel, count),
        out_shape=jax.ShapeDtypeStruct((rows, width), bf16),
        in_specs=[vmem, vmem, vmem, vmem, hbm, hbm],
        out_specs=hbm,
        scratch_shapes=[
            gathered, table, table, columns, win, wout, hidden, partial, from_core, from_y,
            pair_in, single_in, out_buf,
            dma((2,)), dma((PARTS,)), dma((count - 1,)), dma((count - 1,)),
            dma((2 * pieces,)), dma((pieces,)), dma((pieces,)), dma((pieces,)),
        ]
        + [dma((pieces,))] * 6
        + [dma((pieces, tiles))] * 2
        + [dma((pieces,))] * 2
        + [dma((4 * pieces,)), dma((len(PAIRS), PARTS, 2))]
        + [dma((2 * pieces,)), dma((len(SINGLES), PARTS))],
        compiler_params=pltpu.CompilerParams(
            collective_id=0, has_side_effects=True, vmem_limit_bytes=60 * 2**20
        ),
    )(resid, norm_gain[None], expert_ids.T, route_weights.T, w_in, w_out)


def local_wide(resid, norm_gain, expert_ids, route_weights, w_in, w_out):
    token_rows, model_width = resid.shape
    top_count = expert_ids.shape[1]
    ep_devices = lax.axis_size("ep")
    capacity = 3 * token_rows * top_count // (2 * ep_devices)
    weight_in = w_in[0]
    weight_out = w_out[0]
    hidden_units = weight_out.shape[0]
    resid_wide = resid.astype(jnp.float32)
    scale = lax.rsqrt(jnp.mean(resid_wide * resid_wide, axis=-1, keepdims=True) + 1e-06)
    normed = (resid_wide * scale * norm_gain).astype(jnp.bfloat16)
    mix_weights = route_weights / jnp.sum(route_weights, axis=-1, keepdims=True)
    flat_ids = expert_ids.reshape(-1)
    onehot = (flat_ids[:, None] == jnp.arange(ep_devices, dtype=jnp.int32)[None, :]).astype(
        jnp.int32
    )
    position = jnp.sum((jnp.cumsum(onehot, axis=0) - onehot) * onehot, axis=1)
    slot_index = flat_ids * capacity + position
    all_normed, all_ids = (
        lax.all_gather(normed, "ep", axis=0, tiled=True),
        lax.all_gather(expert_ids, "ep", axis=0, tiled=True),
    )
    own_expert = lax.axis_index("ep")
    row_hits = (
        jnp.any(all_ids == own_expert, axis=1).astype(jnp.int32).reshape(ep_devices, token_rows)
    )
    placing = jnp.cumsum(row_hits, axis=1) - row_hits
    target = jnp.where(
        row_hits == 1,
        jnp.arange(ep_devices, dtype=jnp.int32)[:, None] * capacity + placing,
        ep_devices * capacity,
    ).reshape(-1)
    received = (
        jnp.zeros((ep_devices * capacity, model_width), jnp.bfloat16)
        .at[target]
        .set(all_normed, mode="drop")
    )
    block_rows = received.reshape(ep_devices, capacity, model_width)
    rows_flat = block_rows.reshape(-1, model_width)
    projected = jnp.dot(rows_flat, weight_in, preferred_element_type=jnp.float32)
    activated = (jax.nn.silu(projected[:, :hidden_units]) * projected[:, hidden_units:]).astype(
        jnp.bfloat16
    )
    produced = jnp.dot(activated, weight_out, preferred_element_type=jnp.float32).astype(
        jnp.bfloat16
    )
    outputs = produced.reshape(block_rows.shape)
    returned = lax.all_to_all(outputs, "ep", split_axis=0, concat_axis=0, tiled=True).reshape(
        -1, model_width
    )
    picked = returned[slot_index].reshape(token_rows, top_count, model_width).astype(jnp.float32)
    mixed = jnp.sum(mix_weights[:, :, None] * picked, axis=1)
    return (resid_wide + mixed).astype(jnp.bfloat16)


def solution(mesh):
    in_specs = (
        P(("groups", "ep"), None),
        P(),
        P(("groups", "ep"), None),
        P(("groups", "ep"), None),
        P("ep", None, None),
        P("ep", None, None),
    )
    out_specs = P(("groups", "ep"), None)
    return jax.shard_map(local, mesh=mesh, in_specs=in_specs, out_specs=out_specs, check_vma=False)
```

time: 115 us -> 91 us (0.79)
  Pallas kernels: 113 us -> 88.9 us
    pallas_call x1, Pallas kernels: 113 us -> 88.9 us  [local(): pl.pallas_call(functools.partial(moe_kernel, count), out_shape=jax.ShapeD...]
where the time goes in v1:
time: 91 us; the launch traced here: 90.8 us
  Pallas kernels  88.9 us (98%)
  local copies, waits for them, and re-layouts  1.88 us (2%)
    pallas_call x1, Pallas kernels, local(): pl.pallas_call(functools.partial(moe_kernel, count), out_shape=jax.ShapeD...  88.9 us
    unnamed x1, local copies, waits for them, and re-layouts  1.88 us

profile of v1, /device:TPU:0, one launch (start us, length us, event | category | flops | bytes accessed | tf_op | source)
XLA Modules:
  0.0 90.8 jit_solution(14233079346151934507)
XLA Ops:
  0.0 88.9 %shard_map.64 = bf16[128,2048]{1,0:T(8,128)(2,1)} custom-call(bf16[128,2048]{1,0:T(8,128)(2,1)} %resid_ref.1, f32[1,2048]{1,0:T(1,128)} %bitcast.3, s32[8,128]{1,0:T(8,128)} %bitcast.4, f32[8,128]{1,0:T(8,128)} %bitcast.5, bf16[1,2048,1536]{2,1,0:T(8,128)(2,1)} %win_hbm.1, bf16[1,768,2048]{2,1,0:T(8,128)(2,1)} %wout_hbm.1), custom_call_target="tpu_custom_call" | custom-call | tf_op jit(solution)/shard_map/pallas_call | solution.py:418
  88.9 1.9 %copy.8 = bf16[128,2048]{1,0:T(8,128)(2,1)} copy(bf16[128,2048]{1,0:T(8,128)(2,1)} %shard_map.64) | data formatting | bytes 1048576

commit v2 on v1

--- a/solution.py
+++ b/solution.py
@@ -16,31 +16,31 @@
 SINGLES = ("m1", "mB", "t2", "t3", "far")
 
 END_STEPS = (
-    ("zs", 0, "01", (1, 2)), ("yc", 1), ("yc", 2), ("hand", 1), ("zs", 1, "01", (1, 3)),
-    ("xa", 1), ("hand", 2), ("yc", 4), ("zz", 1, "01", (1, 3)), ("yc", 0), ("xb", 1), ("xa", 2),
-    ("xb", 2), ("hand", 4), ("pair", 2, 1, "01", (1, "pA", 0)), ("xa", 4), ("yc", 6), ("hand", 0),
-    ("xb", 4), ("pair", 4, 0, "01", (1, "t2p", 0)), ("yc", 7), ("yc", 5),
-    ("pair", 4, 1, "01", (1, "t2p", 0)), ("hand", 6), ("xa", 6), ("xb", 6), ("hand", 7),
-    ("sy", 6), ("xa", 7), ("xb", 7), ("hand", 5), ("pf", 3), ("pair", 2, 0, "01", (1, "pA", 0)),
-    ("sy", 7), ("xa", 5), ("xb", 5), ("ss", 6, "01", (1, "t3", 0), None), ("c", 3), ("sy", 5),
-    ("xa", 3), ("ss", 7, "01", (1, "t3", 1), None), ("xb", 3), ("sy", 3), ("sy", 1, ("pA", 1, 0)),
-    ("ss", 5, "01", (1, "t2", 1), None), ("xa", 0), ("xb", 0),
-    ("ss", 3, "01", (1, "m1", 1), None), ("sy", 0), ("fin", 1, ("far", 1), ("pA", 1, 1)),
-    ("fin", 0, ("far", 0), ("m1", 0)),
+    ("yc", 0), ("zs", 0, "01", (1, 2)), ("zs", 1, "01", (1, 3)), ("yc", 1), ("yc", 2),
+    ("hand", 0), ("hand", 1), ("zz", 1, "01", (1, 3)), ("xa", 0), ("yc", 4), ("xb", 0),
+    ("hand", 2), ("xa", 2), ("yc", 6), ("xb", 2), ("hand", 4), ("pair", 2, 0, "01", (1, "pA", 0)),
+    ("pair", 2, 1, "01", (1, "pA", 0)), ("yc", 7), ("xa", 4), ("hand", 6), ("xb", 4), ("xa", 6),
+    ("yc", 5), ("xb", 6), ("hand", 7), ("pair", 4, 1, "01", (1, "t2p", 0)),
+    ("pair", 4, 0, "01", (1, "t2p", 0)), ("sy", 6), ("xa", 7), ("xb", 7), ("hand", 5), ("sy", 7),
+    ("xa", 5), ("c", 3), ("pf", 3), ("xb", 5), ("ss", 6, "01", (1, "t3", 0), None), ("sy", 5),
+    ("xa", 3), ("ss", 7, "01", (1, "t3", 1), None), ("xb", 3), ("sy", 3),
+    ("ss", 5, "01", (1, "t2", 1), None), ("xa", 1), ("sy", 0), ("xb", 1), ("sy", 1),
+    ("ss", 3, "01", (1, "m1", 1), None), ("fin", 0, ("far", 0), ("m1", 0)),
+    ("fin", 1, ("far", 1), ("m1", 1)),
 )
 
 INNER_STEPS = (
-    ("zs", 0, "12", (1, 4)), ("zs", 0, "10", (0, 2)), ("yc", 1), ("zs", 1, "12", (1, 5)),
-    ("on", 2, "12", (1, 6)), ("yc", 0), ("hand", 1), ("on", 4, "10", (0, 4)), ("yc", 2),
-    ("on", 5, "10", (0, 5)), ("xa", 1), ("c", 4), ("c", 5), ("on", 3, "12", (1, 7)), ("hand", 0),
-    ("xb", 1), ("yc", 6), ("on", 6, "10", (0, 6)), ("hand", 2), ("pf", 3), ("c", 3), ("xa", 2),
-    ("on", 7, "10", (0, 7)), ("xb", 2), ("hand", 6), ("zz", 0, "12", (1, 4)),
-    ("zz", 1, "10", (0, 3)), ("sy", 2), ("yc", 7), ("xa", 3), ("xb", 3), ("sy", 1),
-    ("zs", 1, "10", (0, 3)), ("zz", 1, "12", (1, 5)), ("xa", 6), ("pf", 4), ("xb", 6), ("xa", 4),
-    ("hand", 7), ("pair", 3, 0, "10", (0, "pA", 1)), ("sy", 6), ("xb", 4),
-    ("ss", 2, "10", (0, "m1", 0), None), ("pair", 4, 1, "12", (1, "pB", 0), ("t2p", 0, 1)),
-    ("xa", 7), ("pf", 5), ("pair", 3, 1, "10", (0, "pA", 1)), ("xb", 7), ("sy", 7),
-    ("pair", 4, 0, "12", (1, "pB", 0), ("t2p", 0, 0)), ("xa", 5), ("xb", 5),
+    ("yc", 1), ("zs", 0, "12", (1, 4)), ("zs", 0, "10", (0, 2)), ("on", 4, "10", (0, 4)),
+    ("on", 2, "12", (1, 6)), ("hand", 1), ("yc", 2), ("xa", 1), ("on", 3, "12", (1, 7)),
+    ("yc", 0), ("on", 6, "10", (0, 6)), ("hand", 2), ("xb", 1), ("xa", 2), ("yc", 6), ("c", 4),
+    ("c", 3), ("zs", 1, "12", (1, 5)), ("pf", 3), ("on", 7, "10", (0, 7)), ("yc", 7), ("xb", 2),
+    ("xa", 3), ("zz", 1, "12", (1, 5)), ("on", 5, "10", (0, 5)), ("xb", 3),
+    ("zs", 1, "10", (0, 3)), ("hand", 0), ("sy", 3), ("hand", 6), ("c", 5),
+    ("zz", 1, "10", (0, 3)), ("sy", 2), ("zz", 0, "12", (1, 4)), ("xa", 6), ("xb", 6), ("sy", 6),
+    ("pf", 4), ("hand", 7), ("sy", 1), ("xa", 4), ("pf", 5), ("xb", 4),
+    ("ss", 3, "10", (0, "m1", 1), None), ("pair", 4, 1, "12", (1, "pB", 0), ("t2p", 0, 1)),
+    ("ss", 2, "10", (0, "m1", 0), None), ("xa", 7), ("xb", 7),
+    ("pair", 4, 0, "12", (1, "pB", 0), ("t2p", 0, 0)), ("xa", 5), ("sy", 7), ("xb", 5),
     ("ss", 6, "110", (0, "far", 0), ("t3", 0)), ("sy", 5, None), ("xa", 0), ("xb", 0),
     ("ss", 7, "110", (0, "far", 1), ("t3", 1)), ("sy", 0, ("pA", 0, 0), ("pB", 0, 0)),
     ("ss", 5, "12", (1, "mB", 1), ("t2", 1)), ("fin", 0, ("pA", 0, 1), ("pB", 0, 1)),

time: 91 us -> 87.5 us (0.962)
  Pallas kernels: 88.9 us -> 85.4 us
    pallas_call x1, Pallas kernels: 88.9 us -> 85.4 us  [local(): pl.pallas_call(functools.partial(moe_kernel, count), out_shape=jax.ShapeD...]
where the time goes in v2:
time: 87.5 us; the launch traced here: 87.3 us
  Pallas kernels  85.4 us (98%)
  local copies, waits for them, and re-layouts  1.88 us (2%)
    pallas_call x1, Pallas kernels, local(): pl.pallas_call(functools.partial(moe_kernel, count), out_shape=jax.ShapeD...  85.4 us
    unnamed x1, local copies, waits for them, and re-layouts  1.88 us

profile of v2, /device:TPU:0, one launch (start us, length us, event | category | flops | bytes accessed | tf_op | source)
XLA Modules:
  0.0 87.3 jit_solution(10020441638282436121)
XLA Ops:
  0.0 85.4 %shard_map.64 = bf16[128,2048]{1,0:T(8,128)(2,1)} custom-call(bf16[128,2048]{1,0:T(8,128)(2,1)} %resid_ref.1, f32[1,2048]{1,0:T(1,128)} %bitcast.3, s32[8,128]{1,0:T(8,128)} %bitcast.4, f32[8,128]{1,0:T(8,128)} %bitcast.5, bf16[1,2048,1536]{2,1,0:T(8,128)(2,1)} %win_hbm.1, bf16[1,768,2048]{2,1,0:T(8,128)(2,1)} %wout_hbm.1), custom_call_target="tpu_custom_call" | custom-call | tf_op jit(solution)/shard_map/pallas_call | solution.py:418
  85.4 1.9 %copy.8 = bf16[128,2048]{1,0:T(8,128)(2,1)} copy(bf16[128,2048]{1,0:T(8,128)(2,1)} %shard_map.64) | data formatting | bytes 1048576
